TPU v7x, 32 devices: a whole 2x2x4 slice. The times are simulated.
32 devices in a mesh: grp: 2 (over y), seq: 4 (over z), head: 4 (over x, core).
Axes of the slice: x: 2, y: 2, z: 4, core: 2. Of those that a mesh axis runs over, the one named last changes fastest.
Arguments:
- queries: bfloat16 [5120, 8192], P(('grp', 'seq'), 'head'), parts along dimension 0, may hold values from -30 to 30, as said below
- keys: bfloat16 [5120, 8192], P(('grp', 'seq'), 'head'), parts along dimension 0, may hold values from -6 to 6
- values: bfloat16 [5120, 8192], P(('grp', 'seq'), 'head'), parts along dimension 0, may hold values from -24 to 24, as said below
- gain: bfloat16 [8192], P('head'), may hold values from 0.25 to 1.75
Outputs:
- output: bfloat16 [5120, 8192], P(('grp', 'seq'), 'head'), parts along dimension 0
There are 2 independent parts, one for each index of `grp`. A program takes and returns all parts, laid end to end along the dimension named above; an argument that names none is the same for every part. Nothing has to cross between parts.
Inputs may be any that keep to these rules, and one draw needn't show every extreme that they name: `queries`: query rows of various sizes. `values`: value features and rows of various sizes.
All inputs are finite; a program needn't handle non-finite values.
Results may differ from a plain program's by a relative error of at most 0.0051.
Values sent between devices are 32-bit elements; how exact they have to be, the bound alone decides.
No kernel may reach another device: no remote copies, remote signals or barrier semaphores. Data moves between devices by JAX's collectives and lax.ppermute only.
A program may use at most 64 MiB of HBM per device.

v0:
```python
import jax
import jax.numpy as jnp
from jax import lax
from jax.sharding import PartitionSpec as P

HEADS = 64
HEAD_DIM = 128


def body(queries, keys, values, gain):
    tokens_here = queries.shape[0]
    heads_here = queries.shape[1] // HEAD_DIM
    queries_split = queries.reshape(tokens_here, heads_here, HEAD_DIM)
    keys_split = keys.reshape(tokens_here, heads_here, HEAD_DIM)
    values_split = values.reshape(tokens_here, heads_here, HEAD_DIM)
    local_state = jnp.einsum(
        "thd,the->hde", keys_split, values_split, preferred_element_type=jnp.float32
    )
    my_index = lax.axis_index("seq")
    piece = lax.all_gather(local_state[None], "seq", axis=0, tiled=True)
    owners = jnp.arange(piece.shape[0], dtype=jnp.int32)
    weights = (owners < my_index).astype(jnp.float32)
    prefix = jnp.sum(piece * weights[:, None, None, None], axis=0)
    positions = jnp.arange(tokens_here)
    causal = positions[:, None] >= positions[None, :]
    scores = jnp.einsum(
        "thd,shd->hts", queries_split, keys_split, preferred_element_type=jnp.float32
    )
    scores = jnp.where(causal[None], scores, jnp.float32(0.0)).astype(jnp.bfloat16)
    intra_term = jnp.einsum(
        "hts,she->the", scores, values_split, preferred_element_type=jnp.float32
    )
    prefix_low = prefix.astype(jnp.bfloat16)
    inter_term = jnp.einsum(
        "thd,hde->the", queries_split, prefix_low, preferred_element_type=jnp.float32
    )
    mixed = (intra_term + inter_term).reshape(tokens_here, heads_here * HEAD_DIM)
    partial_squares = jnp.sum(mixed * mixed, axis=1)
    total_squares = lax.psum(partial_squares, "head")
    factor = lax.rsqrt(total_squares / (HEADS * HEAD_DIM) + 1e-06)
    return (mixed * factor[:, None] * gain.astype(jnp.float32)[None, :]).astype(jnp.bfloat16)


def solution(mesh):
    placed = (
        P(("grp", "seq"), "head"),
        P(("grp", "seq"), "head"),
        P(("grp", "seq"), "head"),
        P("head"),
    )
    return jax.shard_map(
        body, mesh=mesh, in_specs=placed, out_specs=P(("grp", "seq"), "head"), check_vma=False
    )
```

profile of v0, /device:TPU:0, one launch (start us, length us, event | category | flops | bytes accessed | tf_op | source)
XLA Modules:
  0.0 132.1 jit_solution(14653907628350191327)
XLA Ops:
  6.5 0.0 copy-start
  6.5 0.0 all-gather.3.cloned.1.call-start
  6.5 4.5 %copy.17 = bf16[640,2048]{0,1:T(8,128)(2,1)} copy(bf16[640,2048]{1,0:T(8,128)(2,1)} %param.5) | data formatting | bytes 5242880 | tf_op jit(solution)/shard_map/reshape | solution.py:14
  11.1 0.0 copy-start.1
  11.1 4.4 %fusion.2 = f32[16,128,128]{2,1,0:T(8,128)} fusion(bf16[640,16,128]{0,2,1:T(8,128)(2,1)} %bitcast.43, bf16[640,2048]{1,0:T(8,128)(2,1)} %param.6), kind=kOutput, calls=%fused_computation.7 | convolution fusion | flops 335544320 | bytes 6291456 | tf_op jit(solution)/shard_map/thd,the->hde/dot_general | solution.py:16
  15.4 0.0 all-gather.3.cloned.1.call-update
  15.5 0.0 copy-done.1
  15.5 0.1 iota_compare_fusion
  15.6 0.0 copy-done
  15.6 10.9 %fusion = f32[16,640,128]{1,2,0:T(8,128)} fusion(bf16[640,16,128]{0,2,1:T(8,128)(2,1)} %bitcast.44, pred[640,640]{1,0:T(8,128)(4,1)S(1)} %iota_compare_fusion, bf16[640,2048]{1,0:T(8,128)(2,1)} %param.6, bf16[640,2048]{1,0:T(8,128)(2,1)S(1)} %copy-done), kind=kOutput, calls=%fused_computation.5 | convolution fusion | flops 3368550400 | bytes 13516800 | tf_op jit(solution)/shard_map/hts,she->the/dot_general | solution.py:30
  26.5 72.6 %all-gather.3.cloned.1.call-done = f32[64,128,128]{2,1,0:T(8,128)} async-done(((f32[16,128,128]{2,1,0:T(8,128)}), f32[64,128,128]{2,1,0:T(8,128)}) %all-gather.3.cloned.1.call-update) | async-done | bytes 4194320 | tf_op jit(solution)/shard_map/all_gather | solution.py:20
  99.1 2.7 %multiply_reduce_fusion.1 = bf16[16,128,128]{2,1,0:T(8,128)(2,1)S(1)} fusion(f32[4,16,128,128]{3,2,1,0:T(8,128)} %bitcast.42, f32[4]{0:T(128)S(1)} %compare_convert_fusion), kind=kLoop, calls=%fused_computation.4 | loop fusion | flops 1835008 | bytes 4718608 | tf_op jit(solution)/shard_map/reduce_sum | solution.py:23
  101.8 6.0 %multiply_reduce_fusion = (f32[640]{0:T(1024)S(1)}, f32[640,16,128]{0,2,1:T(8,128)}) fusion(bf16[16,128,128]{2,1,0:T(8,128)(2,1)S(1)} %multiply_reduce_fusion.1, f32[16,640,128]{1,2,0:T(8,128)} %fusion, bf16[640,2048]{1,0:T(8,128)(2,1)S(1)} %copy-done), kind=kOutput, calls=%fused_computation.3 | convolution fusion | flops 339475840 | bytes 13634048 | tf_op jit(solution)/shard_map/thd,hde->the/dot_general | solution.py:34
  107.8 6.0 %copy.15 = f32[640,2048]{1,0:T(8,128)} copy(f32[640,2048]{0,1:T(8,128)} %bitcast.41) | data formatting | bytes 10485760 | tf_op jit(solution)/shard_map/reshape | solution.py:37
  113.9 6.9 %psum.7 = f32[640]{0:T(1024)S(1)} all-reduce(f32[640]{0:T(1024)S(1)} %get-tuple-element.5), channel_id=1, replica_groups=mesh['grp'=2,'seq'=4,'head'=4] {'head'}, use_global_device_ids=true, to_apply=%region_2.3 | all-reduce | flops 640 | bytes 5120 | tf_op jit(solution)/shard_map/psum | solution.py:39
  120.7 4.5 %multiply_convert_fusion = bf16[640,2048]{1,0:T(8,128)(2,1)} fusion(f32[640,2048]{1,0:T(8,128)} %copy.15, f32[2048]{0:T(1024)S(1)} %convert_element_type.22, f32[640]{0:T(1024)S(1)} %add_rsqrt_fusion), kind=kLoop, calls=%fused_computation.2 | loop fusion | flops 3932160 | bytes 7875072 | tf_op jit(solution)/shard_map/convert_element_type | solution.py:41
  (3 shorter events, 0.0 us)
Async XLA Ops:
  6.5 9.1 %copy-start = (bf16[640,2048]{1,0:T(8,128)(2,1)S(1)}, bf16[640,2048]{1,0:T(8,128)(2,1)}, u32[]{:S(2)}) copy-start(bf16[640,2048]{1,0:T(8,128)(2,1)} %param.4) | copy-start | bytes 7864324
  6.5 92.5 %all-gather.3.cloned.1.call-start = ((), (), s32[]{:S(2)}) async-start(), calls=%async_computation | async-start | bytes 5242880 | tf_op jit(solution)/shard_map/all_gather | solution.py:20
  11.1 4.4 %copy-start.1 = (bf16[2048]{0:T(1024)(128)(2,1)S(1)}, bf16[2048]{0:T(1024)(128)(2,1)}, u32[]{:S(2)}) copy-start(bf16[2048]{0:T(1024)(128)(2,1)} %param.7) | copy-start | bytes 12292
Sparse Core Ops, SparseCore 0:
  15.6 83.4 all-gather.2
where the time goes:
time: 132 us
  waiting for transfers between devices  72.6 us (55%)
  matrix products  21.3 us (16%)
  between operations  13.4 us (10%)
  local copies, waits for them, and re-layouts  10.6 us (8%)
  other arithmetic  7.33 us (6%)
  blocking collectives  6.86 us (5%)
    all_gather x1, waiting for transfers between devices, body(): piece = lax.all_gather(local_state[None], 'seq', axis=0, tiled=True)  72.6 us
    dot_general x1, matrix products, body(): jnp.einsum('hts,she->the', scores, values_split, preferred_element_type=j...  10.9 us
    psum x1, blocking collectives, body(): total_squares = lax.psum(partial_squares, 'head')  6.86 us
    reshape x1, local copies, waits for them, and re-layouts, body(): (intra_term + inter_term).reshape(tokens_here, heads_here * HEAD_DIM)  6.05 us
    dot_general x1, matrix products, body(): jnp.einsum('thd,hde->the', queries_split, prefix_low, preferred_element_t...  6.03 us
    reshape x1, local copies, waits for them, and re-layouts, body(): keys_split = keys.reshape(tokens_here, heads_here, HEAD_DIM)  4.52 us
    convert_element_type x1, other arithmetic, body(): (mixed * factor[:, None] * gain.astype(jnp.float32)[None, :]).astype(jnp....  4.47 us
    dot_general x1, matrix products, body(): jnp.einsum('thd,the->hde', keys_split, values_split, preferred_element_ty...  4.37 us
  transfers between devices with their start and end apart: 1, of which 1 were waited for; matrix products, arithmetic and copies ran while one was open for 8% of the time, Pallas kernels for 0%

commit v1 on v0

--- a/solution.py
+++ b/solution.py
@@ -17,7 +17,12 @@
         "thd,the->hde", keys_split, values_split, preferred_element_type=jnp.float32
     )
     my_index = lax.axis_index("seq")
-    piece = lax.all_gather(local_state[None], "seq", axis=0, tiled=True)
+    ring = [local_state[None]]
+    for hop in range(3):
+        ring.append(lax.ppermute(ring[-1], "seq", [(dev, (dev + 1) % 4) for dev in range(4)]))
+    piece = jnp.roll(
+        jnp.concatenate(ring[::-1], axis=0), (lax.axis_index("seq") + 1) * ring[0].shape[0], axis=0
+    )
     owners = jnp.arange(piece.shape[0], dtype=jnp.int32)
     weights = (owners < my_index).astype(jnp.float32)
     prefix = jnp.sum(piece * weights[:, None, None, None], axis=0)

time: 132 us -> 118 us (0.89)
  between operations: 13.4 us -> 0.17 us
  local copies, waits for them, and re-layouts: 10.6 us -> 19.9 us
  waiting for transfers between devices: 72.6 us -> 66.3 us
  matrix products: 21.3 us -> 17.8 us
  starting transfers between devices: 0.01 us -> 3.03 us
  other arithmetic: 7.33 us -> 5.15 us
    all_gather x1 -> x0, waiting for transfers between devices: 72.6 us -> none  [body(): piece = lax.all_gather(local_state[None], 'seq', axis=0, tiled=True)]
    ppermute x0 -> x3, waiting for transfers between devices: none -> 66.3 us  [body(): lax.ppermute(ring[-1], 'seq', [(dev, (dev + 1) % 4) for dev in range(4)])]
    unnamed x4 -> x19, local copies, waits for them, and re-layouts: 0.01 us -> 9.22 us
    ppermute x0 -> x3, starting transfers between devices: none -> 3.03 us  [body(): lax.ppermute(ring[-1], 'seq', [(dev, (dev + 1) % 4) for dev in range(4)])]
    dot_general x1, matrix products: 6.03 us -> 3.61 us  [body(): jnp.einsum('thd,hde->the', queries_split, prefix_low, preferred_element_t...]
    reduce_sum x1, other arithmetic: 2.71 us -> 0.54 us  [body(): prefix = jnp.sum(piece * weights[:, None, None, None], axis=0)]
  transfers between devices with their start and end apart: 1 -> 3, of which waited for: 1 -> 3; matrix products, arithmetic and copies ran while one was open for 8% -> 9% of each run, Pallas kernels for 0% -> 0%
where the time goes in v1:
time: 118 us
  waiting for transfers between devices  66.3 us (56%)
  local copies, waits for them, and re-layouts  19.9 us (17%)
  matrix products  17.8 us (15%)
  blocking collectives  5.63 us (5%)
  other arithmetic  5.15 us (4%)
  starting transfers between devices  3.03 us (3%)
    ppermute x3, waiting for transfers between devices, body(): lax.ppermute(ring[-1], 'seq', [(dev, (dev + 1) % 4) for dev in range(4)])  66.3 us
    dot_general x1, matrix products, body(): jnp.einsum('hts,she->the', scores, values_split, preferred_element_type=j...  10.8 us
    unnamed x19, local copies, waits for them, and re-layouts  9.22 us
    reshape x1, local copies, waits for them, and re-layouts, body(): (intra_term + inter_term).reshape(tokens_here, heads_here * HEAD_DIM)  6.04 us
    psum x1, blocking collectives, body(): total_squares = lax.psum(partial_squares, 'head')  5.63 us
    reshape x1, local copies, waits for them, and re-layouts, body(): keys_split = keys.reshape(tokens_here, heads_here, HEAD_DIM)  4.54 us
    convert_element_type x1, other arithmetic, body(): (mixed * factor[:, None] * gain.astype(jnp.float32)[None, :]).astype(jnp....  4.47 us
    dot_general x1, matrix products, body(): jnp.einsum('thd,hde->the', queries_split, prefix_low, preferred_element_t...  3.61 us
  transfers between devices with their start and end apart: 3, of which 3 were waited for; matrix products, arithmetic and copies ran while one was open for 9% of the time, Pallas kernels for 0%

profile of v1, /device:TPU:0, one launch (start us, length us, event | category | flops | bytes accessed | tf_op | source)
XLA Modules:
  0.0 118.0 jit_solution(18232689133772952135)
XLA Ops:
  0.0 0.0 copy-start
  0.0 4.5 %copy.17 = bf16[640,2048]{0,1:T(8,128)(2,1)} copy(bf16[640,2048]{1,0:T(8,128)(2,1)} %param.5) | data formatting | bytes 5242880 | tf_op jit(solution)/shard_map/reshape | solution.py:14
  4.5 3.4 %fusion.16 = f32[1,16,128,128]{3,2,1,0:T(8,128)S(1)} fusion(bf16[640,16,128]{0,2,1:T(8,128)(2,1)} %bitcast.47, bf16[640,2048]{1,0:T(8,128)(2,1)} %param.6), kind=kOutput, calls=%fused_computation.17 | convolution fusion | flops 335544320 | bytes 6291456 | tf_op jit(solution)/shard_map/thd,the->hde/dot_general | solution.py:16
  7.9 0.0 copy-start.1
  7.9 1.0 copy-done.1
  8.9 3.0 %collective-permute-start = (f32[1,16,128,128]{3,2,1,0:T(8,128)S(1)}, f32[1,16,128,128]{3,2,1,0:T(8,128)}, u32[]{:S(2)}, u32[]{:S(2)}) collective-permute-start(f32[1,16,128,128]{3,2,1,0:T(8,128)S(1)} %fusion.16), channel_id=1, source_target_pairs={{0,4},{4,8},{8,12},{12,0},{1,5},{5,9},{9,13},{13,1},{2,6},{6,10},{... | collective-permute-start | bytes 3145736 | tf_op jit(solution)/shard_map/ppermute | solution.py:22
  12.0 25.3 %collective-permute-done = f32[1,16,128,128]{3,2,1,0:T(8,128)} collective-permute-done((f32[1,16,128,128]{3,2,1,0:T(8,128)S(1)}, f32[1,16,128,128]{3,2,1,0:T(8,128)}, u32[]{:S(2)}, u32[]{:S(2)}) %collective-permute-start) | collective-permute-done | bytes 1048608 | tf_op jit(solution)/shard_map/ppermute | solution.py:22
  37.2 0.0 collective-permute-start.1
  37.2 0.0 copy-done.3
  37.3 0.1 iota_compare_fusion
  37.4 26.3 %collective-permute-done.1 = f32[1,16,128,128]{3,2,1,0:T(8,128)} collective-permute-done((f32[1,16,128,128]{3,2,1,0:T(8,128)}, f32[1,16,128,128]{3,2,1,0:T(8,128)}, u32[]{:S(2)}, u32[]{:S(2)}) %collective-permute-start.1) | collective-permute-done | bytes 1048608 | tf_op jit(solution)/shard_map/ppermute | solution.py:22
  63.7 0.0 collective-permute-start.2
  63.7 0.0 copy-done
  63.7 10.8 %fusion = f32[16,640,128]{1,2,0:T(8,128)} fusion(bf16[640,16,128]{0,2,1:T(8,128)(2,1)} %bitcast.48, pred[640,640]{1,0:T(8,128)(4,1)S(1)} %iota_compare_fusion, bf16[640,2048]{1,0:T(8,128)(2,1)} %param.6, bf16[640,2048]{1,0:T(8,128)(2,1)S(1)} %copy-done), kind=kOutput, calls=%fused_computation.5 | convolution fusion | flops 3368550400 | bytes 13516800 | tf_op jit(solution)/shard_map/hts,she->the/dot_general | solution.py:35
  74.5 14.7 %collective-permute-done.2 = f32[1,16,128,128]{3,2,1,0:T(8,128)} collective-permute-done((f32[1,16,128,128]{3,2,1,0:T(8,128)}, f32[1,16,128,128]{3,2,1,0:T(8,128)}, u32[]{:S(2)}, u32[]{:S(2)}) %collective-permute-start.2) | collective-permute-done | bytes 1048608 | tf_op jit(solution)/shard_map/ppermute | solution.py:22
  89.2 1.3 %constant_dynamic-update-slice_fusion.7 = f32[8,16,128,128]{3,2,1,0:T(8,128)S(1)} fusion(f32[1,16,128,128]{3,2,1,0:T(8,128)} %collective-permute-done.2), kind=kLoop, calls=%fused_computation.26 | loop fusion | bytes 2097152
  90.6 1.3 %constant_dynamic-update-slice_fusion.6 = f32[8,16,128,128]{3,2,1,0:T(8,128)S(1)} fusion(f32[8,16,128,128]{3,2,1,0:T(8,128)S(1)} %constant_dynamic-update-slice_fusion.7, f32[1,16,128,128]{3,2,1,0:T(8,128)} %collective-permute-done.1), kind=kLoop, calls=%fused_computation.25 | loop fusion | bytes 2097152
  91.9 1.3 %constant_dynamic-update-slice_fusion.5 = f32[8,16,128,128]{3,2,1,0:T(8,128)S(1)} fusion(f32[8,16,128,128]{3,2,1,0:T(8,128)S(1)} %constant_dynamic-update-slice_fusion.6, f32[1,16,128,128]{3,2,1,0:T(8,128)} %collective-permute-done), kind=kLoop, calls=%fused_computation.24 | loop fusion | bytes 2097152
  93.2 0.0 copy-done.2
  93.2 0.0 slice-start
  93.2 0.1 constant_dynamic-update-slice_fusion.4
  93.3 1.5 %constant_dynamic-update-slice_fusion.3 = f32[8,16,128,128]{3,2,1,0:T(8,128)S(1)} fusion(f32[8,16,128,128]{3,2,1,0:T(8,128)S(1)} %constant_dynamic-update-slice_fusion.4, f32[1,16,128,128]{3,2,1,0:T(8,128)} %collective-permute-done.2), kind=kLoop, calls=%fused_computation.22 | loop fusion | bytes 2097152
  94.8 1.3 %constant_dynamic-update-slice_fusion.2 = f32[8,16,128,128]{3,2,1,0:T(8,128)S(1)} fusion(f32[8,16,128,128]{3,2,1,0:T(8,128)S(1)} %constant_dynamic-update-slice_fusion.3, f32[1,16,128,128]{3,2,1,0:T(8,128)} %collective-permute-done.1), kind=kLoop, calls=%fused_computation.21 | loop fusion | bytes 2097152
  96.1 0.0 slice-start.1
  96.1 1.4 %constant_dynamic-update-slice_fusion.1 = f32[8,16,128,128]{3,2,1,0:T(8,128)S(1)} fusion(f32[8,16,128,128]{3,2,1,0:T(8,128)S(1)} %constant_dynamic-update-slice_fusion.2, f32[1,16,128,128]{3,2,1,0:T(8,128)} %collective-permute-done), kind=kLoop, calls=%fused_computation.20 | loop fusion | bytes 2097152
  97.5 0.1 constant_dynamic-update-slice_fusion
  97.6 0.5 multiply_reduce_fusion.1
  98.2 0.0 slice-done
  98.2 3.6 %multiply_reduce_fusion = (f32[640]{0:T(1024)S(1)}, f32[640,16,128]{0,2,1:T(8,128)}) fusion(bf16[16,128,128]{2,1,0:T(8,128)(2,1)S(1)} %multiply_reduce_fusion.1, f32[16,640,128]{1,2,0:T(8,128)S(1)} %bitcast.46, bf16[640,2048]{1,0:T(8,128)(2,1)S(1)} %copy-done), kind=kOutput, calls=%fused_computation.3 | convolution fusion | flops 339475840 | bytes 13634048 | tf_op jit(solution)/shard_map/thd,hde->the/dot_general | solution.py:39
  101.8 6.0 %copy.15 = f32[640,2048]{1,0:T(8,128)} copy(f32[640,2048]{0,1:T(8,128)} %bitcast.44) | data formatting | bytes 10485760 | tf_op jit(solution)/shard_map/reshape | solution.py:42
  107.9 5.6 %psum.7 = f32[640]{0:T(1024)S(1)} all-reduce(f32[640]{0:T(1024)S(1)} %get-tuple-element.5), channel_id=1, replica_groups=mesh['grp'=2,'seq'=4,'head'=4] {'head'}, use_global_device_ids=true, to_apply=%region_2.3 | all-reduce | flops 640 | bytes 5120 | tf_op jit(solution)/shard_map/psum | solution.py:44
  113.5 4.5 %multiply_convert_fusion = bf16[640,2048]{1,0:T(8,128)(2,1)} fusion(f32[640,2048]{1,0:T(8,128)} %copy.15, f32[2048]{0:T(1024)S(1)} %convert_element_type.22, f32[640]{0:T(1024)S(1)} %add_rsqrt_fusion), kind=kLoop, calls=%fused_computation.2 | loop fusion | flops 3932160 | bytes 7875072 | tf_op jit(solution)/shard_map/convert_element_type | solution.py:46
  (7 shorter events, 0.0 us)
Async XLA Ops:
  0.0 63.7 %copy-start = (bf16[640,2048]{1,0:T(8,128)(2,1)S(1)}, bf16[640,2048]{1,0:T(8,128)(2,1)}, u32[]{:S(2)}) copy-start(bf16[640,2048]{1,0:T(8,128)(2,1)} %param.4) | copy-start | bytes 7864324
  0.0 37.2 %copy-start.3 = (bf16[2048]{0:T(1024)(128)(2,1)S(1)}, bf16[2048]{0:T(1024)(128)(2,1)}, u32[]{:S(2)}) copy-start(bf16[2048]{0:T(1024)(128)(2,1)} %param.7) | copy-start | bytes 12292
  7.9 1.0 copy-start.1
  8.9 28.3 %collective-permute-start = (f32[1,16,128,128]{3,2,1,0:T(8,128)S(1)}, f32[1,16,128,128]{3,2,1,0:T(8,128)}, u32[]{:S(2)}, u32[]{:S(2)}) collective-permute-start(f32[1,16,128,128]{3,2,1,0:T(8,128)S(1)} %fusion.16), channel_id=1, source_target_pairs={{0,4},{4,8},{8,12},{12,0},{1,5},{5,9},{9,13},{13,1},{2,6},{6,10},{... | collective-permute-start | bytes 3145736 | tf_op jit(solution)/shard_map/ppermute | solution.py:22
  37.2 26.5 %collective-permute-start.1 = (f32[1,16,128,128]{3,2,1,0:T(8,128)}, f32[1,16,128,128]{3,2,1,0:T(8,128)}, u32[]{:S(2)}, u32[]{:S(2)}) collective-permute-start(f32[1,16,128,128]{3,2,1,0:T(8,128)} %collective-permute-done), channel_id=1, source_target_pairs={{0,4},{4,8},{8,12},{12,0},{1,5},{5,9},{9,13},{13,1},{2,6},{6,10},{... | collective-permute-start | bytes 3145736 | tf_op jit(solution)/shard_map/ppermute | solution.py:22
  63.7 25.5 %collective-permute-start.2 = (f32[1,16,128,128]{3,2,1,0:T(8,128)}, f32[1,16,128,128]{3,2,1,0:T(8,128)}, u32[]{:S(2)}, u32[]{:S(2)}) collective-permute-start(f32[1,16,128,128]{3,2,1,0:T(8,128)} %collective-permute-done.1), channel_id=1, source_target_pairs={{0,4},{4,8},{8,12},{12,0},{1,5},{5,9},{9,13},{13,1},{2,6},{6,10},{... | collective-permute-start | bytes 3145736 | tf_op jit(solution)/shard_map/ppermute | solution.py:22
  74.5 18.7 %copy-start.2 = (f32[1,16,128,128]{3,2,1,0:T(8,128)S(1)}, f32[1,16,128,128]{3,2,1,0:T(8,128)}, u32[]{:S(2)}) copy-start(f32[1,16,128,128]{3,2,1,0:T(8,128)} %copy-done.1) | copy-start | bytes 3145732
  93.2 5.0 %slice-start = ((s8[5242880]{0:T(1024)(128)(4,1)}), s8[4194304]{0:T(1024)(128)(4,1)S(1)}, s32[]{:S(2)}) async-start(s8[5242880]{0:T(1024)(128)(4,1)} %bitcast.45), calls=%async_computation | async-start | bytes 8388608
  96.1 2.1 %slice-start.1 = ((s8[5242880]{0:T(1024)(128)(4,1)}), s8[1048576]{0:T(1024)(128)(4,1)S(1)}, s32[]{:S(2)}) async-start(s8[5242880]{0:T(1024)(128)(4,1)} %bitcast.45), calls=%async_computation.1 | async-start | bytes 2097152
